TPU v7x, 256 devices: a whole 4x4x8 slice. The times are simulated.
256 devices in a mesh: replica: 16 (over z, core), mp: 16 (over y, x).
Axes of the slice: x: 4, y: 4, z: 8, core: 2. Of those that a mesh axis runs over, the one named last changes fastest.
Arguments:
- gradients: bfloat16 [16, 8, 768, 3072], P('replica', None, 'mp'), may hold values from -6 to 6
- feedback: bfloat16 [16, 8, 768, 3072], P('replica', None, 'mp'), may hold values from -4 to 4
- right_init: bfloat16 [8, 3072, 32], replicated, may hold values from -0.109375 to 0.109375
- gram_root: float32 [8, 32, 32], replicated, as said below
- owners: int32 [8], replicated, may hold values from 0 to 15, as said below
- momentum: float32 [16, 1, 768, 3072], P('mp', None, 'replica'), may hold values from -4 to 4
- master_weights: float32 [16, 1, 768, 3072], P('mp', None, 'replica'), may hold values from -1.5 to 1.5
- vector_grads: float32 [16, 10752], P('replica', 'mp'), may hold values from -6 to 6
- vector_momentum: float32 [10752], P('mp'), may hold values from -6 to 6
- vector_params: float32 [10752], P('mp'), may hold values from -6 to 6
Outputs:
- new_feedback: bfloat16 [16, 8, 768, 3072], P('replica', None, 'mp')
- new_momentum: float32 [16, 1, 768, 3072], P('mp', None, 'replica')
- new_master: float32 [16, 1, 768, 3072], P('mp', None, 'replica')
- new_weights: bfloat16 [8, 768, 3072], P(None, 'replica')
- new_vector_momentum: float32 [10752], P('mp')
- new_vector_params: float32 [10752], P('mp')
Inputs may be any that keep to these rules, and one draw needn't show every extreme that they name: `owners`: every matrix has one owner; no owner holds more than 1 of the 8 matrices, and one owner holds exactly 1. `gram_root`: each matrix is the identity plus off-diagonal terms, times a positive scale.
All inputs are finite; a program needn't handle non-finite values.
Results may differ from a plain program's by a relative error of at most 0.007.
Values may be sent and summed in bfloat16 or wider, within the bound.
A program may use at most 192 MiB of HBM per device.

v0:
```python
import jax
import jax.numpy as jnp
from jax import lax
from jax.sharding import PartitionSpec as P


def per_device(
    gradients,
    feedback,
    right_init,
    gram_root,
    owners,
    momentum,
    master_weights,
    vector_grads,
    vector_momentum,
    vector_params,
):
    highest = lax.Precision.HIGHEST
    compensated = (gradients[0].astype(jnp.float32) + feedback[0].astype(jnp.float32)).astype(
        jnp.bfloat16
    )
    owner_count = lax.axis_size("mp")
    capacity = momentum.shape[1]
    matrices = owners.shape[0]
    replica_rows = momentum.shape[2]
    mp_index = lax.axis_index("mp")
    replica_index = lax.axis_index("replica")
    same_owner = owners[:, None] == owners[None, :]
    earlier = jnp.arange(matrices)[:, None] < jnp.arange(matrices)[None, :]
    ranks = jnp.sum((same_owner & earlier).astype(jnp.int32), axis=0)
    slots = owners * capacity + ranks
    mine = slots[None, :] == (mp_index * capacity + jnp.arange(capacity))[:, None]
    has = jnp.any(mine, axis=1)
    chosen = jnp.argmax(mine, axis=1)
    left_terms = jnp.einsum(
        "kmn,knr->kmr", compensated, right_init, preferred_element_type=jnp.float32
    )
    left_sum = lax.psum(left_terms, "replica")
    left_rows = jnp.einsum("kmr,krs->kms", left_sum, gram_root, precision=highest).astype(
        jnp.bfloat16
    )
    right_terms = jnp.einsum(
        "kmn,kms->kns", compensated, left_rows, preferred_element_type=jnp.float32
    )
    right_part = lax.psum_scatter(right_terms.reshape(-1), "mp", scatter_dimension=0, tiled=True)
    right_part = lax.psum(right_part, "replica")
    right_new = lax.all_gather(right_part.astype(jnp.bfloat16), "mp", axis=0, tiled=True).reshape(
        right_terms.shape
    )
    left_all = lax.all_gather(left_rows, "mp", axis=1, tiled=True)
    approx_rows = jnp.einsum(
        "kms,kns->kmn", left_rows, right_new, preferred_element_type=jnp.float32
    )
    new_feedback = (compensated.astype(jnp.float32) - approx_rows).astype(jnp.bfloat16)
    scale = has.astype(jnp.float32)[:, None, None]
    left_chosen = (
        lax.dynamic_slice_in_dim(
            left_all[chosen], replica_index * replica_rows, replica_rows, 1
        ).astype(jnp.float32)
        * scale
    )
    right_chosen = right_new[chosen].astype(jnp.float32) * scale
    approx_slots = jnp.einsum("cmr,cnr->cmn", left_chosen, right_chosen, precision=highest)
    new_momentum = 0.9 * momentum[0] + approx_slots
    new_master = master_weights[0] - 0.1 * new_momentum
    master_narrow = new_master.astype(jnp.bfloat16)
    weight_slots = lax.all_gather(master_narrow, "mp", axis=0, tiled=True)
    new_weights = jnp.take(weight_slots, slots, axis=0)
    vector_total = lax.psum(vector_grads[0], "replica")
    new_vector_momentum = 0.9 * vector_momentum + vector_total
    new_vector_params = vector_params - 0.1 * new_vector_momentum
    return (
        new_feedback[None],
        new_momentum[None],
        new_master[None],
        new_weights,
        new_vector_momentum,
        new_vector_params,
    )


def solution(mesh):
    return jax.shard_map(
        per_device,
        mesh=mesh,
        in_specs=(
            P("replica", None, "mp", None),
            P("replica", None, "mp", None),
            P(),
            P(),
            P(),
            P("mp", None, "replica", None),
            P("mp", None, "replica", None),
            P("replica", "mp"),
            P("mp"),
            P("mp"),
        ),
        out_specs=(
            P("replica", None, "mp", None),
            P("mp", None, "replica", None),
            P("mp", None, "replica", None),
            P(None, "replica", None),
            P("mp"),
            P("mp"),
        ),
        check_vma=False,
    )
```

profile of v0, /device:TPU:1, one launch (start us, length us, event | category | flops | bytes accessed | tf_op | source)
XLA Modules:
  0.0 369.8 jit_solution(15668243150370292519)
XLA Ops:
  7.2 0.0 copy-start
  7.2 0.0 all-reduce.5.cloned.1.call-start
  7.2 1.3 copy-done
  8.6 3.1 fusion.14
  11.7 49.7 %psum.21 = f32[8,48,32]{1,2,0:T(8,128)S(1)} all-reduce(f32[8,48,32]{1,2,0:T(8,128)S(1)} %fusion.14), channel_id=1, replica_groups=mesh['replica'=16,'mp'=16] {'replica'}, use_global_device_ids=true, to_apply=%region_0.0 | all-reduce | flops 12288 | bytes 98304 | tf_op jit(solution)/shard_map/psum | solution.py:39
  61.4 0.4 convolution_convert_fusion
  61.8 9.0 %fusion.12 = f32[8,3072,32]{2,1,0:T(8,128)} fusion(bf16[8,48,32]{1,2,0:T(8,128)(2,1)S(1)} %convolution_convert_fusion, bf16[1,8,48,3072]{3,2,1,0:T(8,128)(2,1)} %param.11, bf16[1,8,48,3072]{3,2,1,0:T(8,128)(2,1)} %param.10), kind=kOutput, calls=%fused_computation.29 | convolution fusion | flops 80216064 | bytes 7888896 | tf_op jit(solution)/shard_map/kmn,kms->kns/dot_general | solution.py:43
  70.8 9.4 %reshape.76 = f32[786432]{0:T(1024)} reshape(f32[8,3072,32]{2,1,0:T(8,128)} %fusion.12) | data formatting | bytes 6291456 | tf_op jit(solution)/shard_map/reshape | solution.py:46
  80.2 0.0 all-reduce.5.cloned.1.call-update
  80.2 0.0 all-gather.4.cloned.1.call-start
  80.3 0.6 copy-done.9
  80.9 0.6 dynamic-slice.8
  82.1 104.3 %all-reduce.5.cloned.1.call-done = f32[786432]{0:T(1024)} async-done(((f32[786432]{0:T(1024)}), f32[786432]{0:T(1024)}) %all-reduce.5.cloned.1.call-update) | async-done | bytes 3145744
  186.4 0.9 dynamic-slice.9
  187.3 48.4 %all-reduce.6 = (bf16[49152]{0:T(1024)(128)(2,1)}, f32[672]{0:T(1024)S(1)}) all-reduce(f32[49152]{0:T(1024)S(1)} %dynamic-slice.9, f32[672]{0:T(1024)S(1)} %reduce.20), channel_id=1, replica_groups=mesh['replica'=16,'mp'=16] {'replica'}, use_global_device_ids=true, to_apply=%region_2.0 | all-reduce | flops 49824 | bytes 300288 | tf_op jit(solution)/shard_map/psum | solution.py:47
  235.7 0.0 all-gather.4.cloned.1.call-update
  235.7 0.0 all-gather.6.cloned.1.call-start
  235.8 0.1 copy.27
  235.9 0.1 convert_reduce_fusion
  236.0 0.7 bitcast_reduce_fusion
  238.0 0.6 compare_and_fusion
  239.9 21.6 %all_gather.10 = bf16[8,768,32]{2,0,1:T(8,128)(2,1)S(1)} all-gather(bf16[8,48,32]{2,0,1:T(8,128)(2,1)S(1)} %copy.27), channel_id=1, replica_groups=mesh['replica'=16,'mp'=16] {'mp'}, dimensions={1}, use_global_device_ids=true | all-gather | bytes 417792 | tf_op jit(solution)/shard_map/all_gather | solution.py:51
  261.5 22.4 %all-gather.4.cloned.1.call-done = bf16[786432]{0:T(1024)(128)(2,1)} async-done(((bf16[49152]{0:T(1024)(128)(2,1)}), bf16[786432]{0:T(1024)(128)(2,1)}) %all-gather.4.cloned.1.call-update) | async-done | bytes 1572880 | tf_op jit(solution)/shard_map/all_gather | solution.py:48
  283.9 7.8 %reshape.77 = bf16[8,3072,32]{2,1,0:T(8,128)(2,1)} reshape(bf16[786432]{0:T(1024)(128)(2,1)} %all-gather.4.cloned.1.call-done) | data formatting | bytes 3145728 | tf_op jit(solution)/shard_map/reshape | solution.py:48
  291.8 3.0 convolution_add_fusion
  294.8 1.1 fusion.7
  295.9 0.0 all-gather.6.cloned.1.call-update
  295.9 0.6 multiply_subtract_fusion
  296.5 7.9 %fusion = bf16[1,8,48,3072]{3,2,1,0:T(8,128)(2,1)} fusion(bf16[8,48,32]{1,2,0:T(8,128)(2,1)S(1)} %convolution_convert_fusion, bf16[8,3072,32]{2,1,0:T(8,128)(2,1)} %reshape.77, bf16[1,8,48,3072]{3,2,1,0:T(8,128)(2,1)} %param.11, bf16[1,8,48,3072]{3,2,1,0:T(8,128)(2,1)} %param.10), kind=kOutput, calls=%fused_computation.3 | convolution fusion | flops 83755008 | bytes 8675328 | tf_op jit(solution)/shard_map/kms,kns->kmn/dot_general | solution.py:52
  304.4 51.0 %all-gather.6.cloned.1.call-done = bf16[768,3072]{1,0:T(8,128)(2,1)} async-done(((bf16[48,3072]{1,0:T(8,128)(2,1)}), bf16[768,3072]{1,0:T(8,128)(2,1)}) %all-gather.6.cloned.1.call-update) | async-done | bytes 4718608 | tf_op jit(solution)/shard_map/all_gather | solution.py:68
  355.4 4.4 %gather_fusion = bf16[8,48,3072]{2,1,0:T(8,128)(2,1)} fusion(bf16[16,48,3072]{2,1,0:T(8,128)(2,1)} %bitcast.36, s32[1024]{0:T(1024)S(1)} %pad_clamp_fusion), kind=kCustom, calls=%fused_computation | custom fusion | bytes 4718624 | tf_op jit(solution)/shard_map/jit(_take)/gather | solution.py:69
  359.9 3.4 broadcast_select_fusion
  (20 shorter events, 0.1 us)
Async XLA Ops:
  7.2 1.4 copy-start
  7.2 54.2 %copy-start.4 = (f32[8,32,32]{2,1,0:T(8,128)S(1)}, f32[8,32,32]{2,1,0:T(8,128)}, u32[]{:S(2)}) copy-start(f32[8,32,32]{2,1,0:T(8,128)} %param.13) | copy-start | bytes 98308
  7.2 179.2 %all-reduce.5.cloned.1.call-start = ((), (), s32[]{:S(2)}) async-start(), calls=%async_computation.2 | async-start | bytes 6291456
  80.2 0.7 copy-start.9
  80.2 1.9 copy-start.7
  80.2 155.7 %copy-start.8 = (s32[8]{0:T(128)S(1)}, s32[8]{0:T(128)}, u32[]{:S(2)}) copy-start(s32[8]{0:T(128)} %param.14) | copy-start | bytes 100
  80.2 203.7 %all-gather.4.cloned.1.call-start = ((), (), s32[]{:S(2)}) async-start(), calls=%async_computation | async-start | bytes 1671168 | tf_op jit(solution)/shard_map/all_gather | solution.py:48
  235.7 119.7 %all-gather.6.cloned.1.call-start = ((), (), s32[]{:S(2)}) async-start(), calls=%async_computation.1 | async-start | bytes 5013504 | tf_op jit(solution)/shard_map/all_gather | solution.py:68
  261.5 30.2 %copy-start.2 = (f32[1,1,48,3072]{3,2,1,0:T(8,128)S(1)}, f32[1,1,48,3072]{3,2,1,0:T(8,128)}, u32[]{:S(2)}) copy-start(f32[1,1,48,3072]{3,2,1,0:T(8,128)} %param.15) | copy-start | bytes 1769476
  291.7 3.0 copy-start.3
  291.8 4.1 %copy-start.5 = (f32[672]{0:T(1024)S(1)}, f32[672]{0:T(1024)}, u32[]{:S(2)}) copy-start(f32[672]{0:T(1024)} %param.19) | copy-start | bytes 8068
  291.8 4.2 %copy-start.6 = (f32[672]{0:T(1024)S(1)}, f32[672]{0:T(1024)}, u32[]{:S(2)}) copy-start(f32[672]{0:T(1024)} %param.18) | copy-start | bytes 8068
  294.8 9.7 %copy-start.1 = (f32[48,3072]{1,0:T(8,128)}, f32[48,3072]{1,0:T(8,128)S(1)}, u32[]{:S(2)}) copy-start(f32[48,3072]{1,0:T(8,128)S(1)} %convolution_add_fusion) | copy-start | bytes 1769476
Sparse Core Ops, SparseCore 0:
  80.3 106.0 all-reduce.4
  235.8 48.0 all-gather.3
  296.0 59.3 all-gather.5
where the time goes:
time: 370 us
  waiting for transfers between devices  178 us (48%)
  blocking collectives  120 us (32%)
  local copies, waits for them, and re-layouts  25.3 us (7%)
  matrix products  23.4 us (6%)
  between operations  17.2 us (5%)
  other arithmetic  6.49 us (2%)
    unnamed x4, waiting for transfers between devices  104 us
    all_gather x1, waiting for transfers between devices, per_device(): weight_slots = lax.all_gather(master_narrow, 'mp', axis=0, tiled=True)  51 us
    psum x1, blocking collectives, per_device(): left_sum = lax.psum(left_terms, 'replica')  49.7 us
    psum x1, blocking collectives, per_device(): right_part = lax.psum(right_part, 'replica')  48.4 us
    all_gather x1, waiting for transfers between devices, per_device(): lax.all_gather(right_part.astype(jnp.bfloat16), 'mp', axis=0, tiled=True)  22.4 us
    all_gather x1, blocking collectives, per_device(): left_all = lax.all_gather(left_rows, 'mp', axis=1, tiled=True)  21.6 us
    reshape x1, local copies, waits for them, and re-layouts, per_device(): right_terms.reshape(-1)  9.41 us
    dot_general x1, matrix products, per_device(): jnp.einsum('kmn,kms->kns', compensated, left_rows, preferred_element_type...  8.99 us
  transfers between devices with their start and end apart: 3, of which 3 were waited for; matrix products, arithmetic and copies ran while one was open for 3% of the time, Pallas kernels for 0%

commit v1 on v0

--- a/solution.py
+++ b/solution.py
@@ -2,6 +2,24 @@
 import jax.numpy as jnp
 from jax import lax
 from jax.sharding import PartitionSpec as P
+
+
+def gather_around(shard, axis, dim):
+    ways, here, lap = (lax.axis_size(axis), lax.axis_index(axis), shard.shape[dim])
+    shape = [n * ways if d == dim else n for d, n in enumerate(shard.shape)]
+    full = lax.dynamic_update_slice_in_dim(
+        jnp.zeros(shape, shard.dtype), shard, here * lap, axis=dim
+    )
+    going_up = going_down = shard
+    for far in range(1, ways // 2 + 1):
+        going_up = lax.ppermute(going_up, axis, [(d, (d + 1) % ways) for d in range(ways)])
+        full = lax.dynamic_update_slice_in_dim(full, going_up, (here - far) % ways * lap, axis=dim)
+        if 2 * far < ways:
+            going_down = lax.ppermute(going_down, axis, [(d, (d - 1) % ways) for d in range(ways)])
+            full = lax.dynamic_update_slice_in_dim(
+                full, going_down, (here + far) % ways * lap, axis=dim
+            )
+    return full
 
 
 def per_device(
@@ -65,7 +83,7 @@
     new_momentum = 0.9 * momentum[0] + approx_slots
     new_master = master_weights[0] - 0.1 * new_momentum
     master_narrow = new_master.astype(jnp.bfloat16)
-    weight_slots = lax.all_gather(master_narrow, "mp", axis=0, tiled=True)
+    weight_slots = gather_around(master_narrow, "mp", 0)
     new_weights = jnp.take(weight_slots, slots, axis=0)
     vector_total = lax.psum(vector_grads[0], "replica")
     new_vector_momentum = 0.9 * vector_momentum + vector_total

time: 370 us -> 402 us (1.086)
  the two profiles are of different devices: /device:TPU:1 before, /device:TPU:32 now
where the time goes in v1:
time: 402 us; the launch traced here: 401 us
  waiting for transfers between devices  156 us (39%)
  blocking collectives  122 us (30%)
  local copies, waits for them, and re-layouts  38.7 us (10%)
  starting transfers between devices  38.2 us (10%)
  matrix products  20.9 us (5%)
  between operations  17.8 us (4%)
  other arithmetic  7.21 us (2%)
    unnamed x3, waiting for transfers between devices  106 us
    psum x1, blocking collectives, per_device(): left_sum = lax.psum(left_terms, 'replica')  48.3 us
    psum x1, blocking collectives, per_device(): right_part = lax.psum(right_part, 'replica')  47.7 us
    ppermute x7, starting transfers between devices, gather_around(): lax.ppermute(going_down, axis, [(d, (d - 1) % ways) for d in range(ways)])  37.1 us
    ppermute x8, waiting for transfers between devices, gather_around(): lax.ppermute(going_up, axis, [(d, (d + 1) % ways) for d in range(ways)])  32 us
    all_gather x1, blocking collectives, per_device(): left_all = lax.all_gather(left_rows, 'mp', axis=1, tiled=True)  25.7 us
    all_gather x1, waiting for transfers between devices, per_device(): lax.all_gather(right_part.astype(jnp.bfloat16), 'mp', axis=0, tiled=True)  18.5 us
    reshape x1, local copies, waits for them, and re-layouts, per_device(): right_terms.reshape(-1)  9.44 us
  transfers between devices with their start and end apart: 17, of which 11 were waited for; matrix products, arithmetic and copies ran while one was open for 5% of the time, Pallas kernels for 0%

profile of v1, /device:TPU:32, one launch (start us, length us, event | category | flops | bytes accessed | tf_op | source)
XLA Modules:
  0.0 400.9 jit_solution(10037012128521519264)
XLA Ops:
  7.2 1.3 copy-done
  8.6 3.1 fusion.13
  11.7 48.3 %psum.21 = f32[8,48,32]{1,2,0:T(8,128)S(1)} all-reduce(f32[8,48,32]{1,2,0:T(8,128)S(1)} %fusion.13), channel_id=1, replica_groups=mesh['replica'=16,'mp'=16] {'replica'}, use_global_device_ids=true, to_apply=%region_0.0 | all-reduce | flops 12288 | bytes 98304 | tf_op jit(solution)/shard_map/psum | solution.py:57
  60.4 8.9 %fusion.11 = f32[8,3072,32]{2,1,0:T(8,128)} fusion(bf16[8,48,32]{1,2,0:T(8,128)(2,1)S(1)} %convolution_convert_fusion, bf16[1,8,48,3072]{3,2,1,0:T(8,128)(2,1)} %param.11, bf16[1,8,48,3072]{3,2,1,0:T(8,128)(2,1)} %param.10), kind=kOutput, calls=%fused_computation.45 | convolution fusion | flops 80216064 | bytes 7888896 | tf_op jit(solution)/shard_map/kmn,kms->kns/dot_general | solution.py:61
  69.4 9.4 %reshape.76 = f32[786432]{0:T(1024)} reshape(f32[8,3072,32]{2,1,0:T(8,128)} %fusion.11) | data formatting | bytes 6291456 | tf_op jit(solution)/shard_map/reshape | solution.py:64
  80.2 105.6 %all-reduce.5.cloned.1.call-done = f32[786432]{0:T(1024)} async-done(((f32[786432]{0:T(1024)}), f32[786432]{0:T(1024)}) %all-reduce.5.cloned.1.call-update) | async-done | bytes 3145744
  185.7 0.9 dynamic-slice.9
  186.7 47.7 %all-reduce.6 = (bf16[49152]{0:T(1024)(128)(2,1)}, f32[672]{0:T(1024)S(1)}) all-reduce(f32[49152]{0:T(1024)S(1)} %dynamic-slice.9, f32[672]{0:T(1024)S(1)} %reduce.20), channel_id=1, replica_groups=mesh['replica'=16,'mp'=16] {'replica'}, use_global_device_ids=true, to_apply=%region_2.0 | all-reduce | flops 49824 | bytes 300288 | tf_op jit(solution)/shard_map/psum | solution.py:65
  238.9 25.7 %all_gather.7 = bf16[8,768,32]{2,0,1:T(8,128)(2,1)S(1)} all-gather(bf16[8,48,32]{2,0,1:T(8,128)(2,1)S(1)} %copy.27), channel_id=1, replica_groups=mesh['replica'=16,'mp'=16] {'mp'}, dimensions={1}, use_global_device_ids=true | all-gather | bytes 417792 | tf_op jit(solution)/shard_map/all_gather | solution.py:69
  265.3 18.5 %all-gather.2.cloned.1.call-done = bf16[786432]{0:T(1024)(128)(2,1)} async-done(((bf16[49152]{0:T(1024)(128)(2,1)}), bf16[786432]{0:T(1024)(128)(2,1)}) %all-gather.2.cloned.1.call-update) | async-done | bytes 1572880 | tf_op jit(solution)/shard_map/all_gather | solution.py:66
  283.8 7.8 %reshape.77 = bf16[8,3072,32]{2,1,0:T(8,128)(2,1)} reshape(bf16[786432]{0:T(1024)(128)(2,1)} %all-gather.2.cloned.1.call-done) | data formatting | bytes 3145728 | tf_op jit(solution)/shard_map/reshape | solution.py:66
  291.7 3.1 convolution_add_fusion
  294.8 1.0 fusion.7
  295.8 2.8 broadcast_in_dim.39
  299.4 1.1 collective-permute-start
  300.5 4.3 %collective-permute-start.1 = (bf16[1,48,3072]{2,1,0:T(8,128)(2,1)S(1)}, bf16[1,48,3072]{2,1,0:T(8,128)(2,1)S(1)}, u32[]{:S(2)}, u32[]{:S(2)}) collective-permute-start(bf16[1,48,3072]{2,1,0:T(8,128)(2,1)S(1)} %get-tuple-element.37), channel_id=1, source_target_pairs={{0,15},{1,0},{2,1},{3,2},{4,3},{5,4},{6,5},{7,6},{8,7},{9,8},{10,9... | collective-permute-start | bytes 884744 | tf_op jit(solution)/shard_map/ppermute | solution.py:18
  304.7 5.4 %fusion = bf16[1,8,48,3072]{3,2,1,0:T(8,128)(2,1)} fusion(bf16[8,48,32]{1,2,0:T(8,128)(2,1)S(1)} %convolution_convert_fusion, bf16[8,3072,32]{2,1,0:T(8,128)(2,1)S(1)} %copy-done.1, bf16[1,8,48,3072]{3,2,1,0:T(8,128)(2,1)S(1)} %copy-done.2, bf16[1,8,48,3072]{3,2,1,0:T(8,128)(2,1)} %param.10), kind=kOutput, calls=%fused_computation.3 | convolution fusion | flops 83755008 | bytes 8675328 | tf_op jit(solution)/shard_map/kms,kns->kmn/dot_general | solution.py:70
  310.5 5.3 %collective-permute-start.3 = (bf16[1,48,3072]{2,1,0:T(8,128)(2,1)S(1)}, bf16[1,48,3072]{2,1,0:T(8,128)(2,1)S(1)}, u32[]{:S(2)}, u32[]{:S(2)}) collective-permute-start(bf16[1,48,3072]{2,1,0:T(8,128)(2,1)S(1)} %collective-permute-done.1), channel_id=1, source_target_pairs={{0,15},{1,0},{2,1},{3,2},{4,3},{5,4},{6,5},{7,6},{8,7},{9,8},{10,9... | collective-permute-start | bytes 884744 | tf_op jit(solution)/shard_map/ppermute | solution.py:18
  317.3 3.4 collective-permute-done.2
  320.7 5.3 %collective-permute-start.5 = (bf16[1,48,3072]{2,1,0:T(8,128)(2,1)S(1)}, bf16[1,48,3072]{2,1,0:T(8,128)(2,1)S(1)}, u32[]{:S(2)}, u32[]{:S(2)}) collective-permute-start(bf16[1,48,3072]{2,1,0:T(8,128)(2,1)S(1)} %collective-permute-done.3), channel_id=1, source_target_pairs={{0,15},{1,0},{2,1},{3,2},{4,3},{5,4},{6,5},{7,6},{8,7},{9,8},{10,9... | collective-permute-start | bytes 884744 | tf_op jit(solution)/shard_map/ppermute | solution.py:18
  327.6 3.2 collective-permute-done.4
  330.8 5.3 %collective-permute-start.7 = (bf16[1,48,3072]{2,1,0:T(8,128)(2,1)S(1)}, bf16[1,48,3072]{2,1,0:T(8,128)(2,1)S(1)}, u32[]{:S(2)}, u32[]{:S(2)}) collective-permute-start(bf16[1,48,3072]{2,1,0:T(8,128)(2,1)S(1)} %collective-permute-done.5), channel_id=1, source_target_pairs={{0,15},{1,0},{2,1},{3,2},{4,3},{5,4},{6,5},{7,6},{8,7},{9,8},{10,9... | collective-permute-start | bytes 884744 | tf_op jit(solution)/shard_map/ppermute | solution.py:18
  337.6 3.2 collective-permute-done.6
  340.8 5.3 %collective-permute-start.9 = (bf16[1,48,3072]{2,1,0:T(8,128)(2,1)S(1)}, bf16[1,48,3072]{2,1,0:T(8,128)(2,1)S(1)}, u32[]{:S(2)}, u32[]{:S(2)}) collective-permute-start(bf16[1,48,3072]{2,1,0:T(8,128)(2,1)S(1)} %collective-permute-done.7), channel_id=1, source_target_pairs={{0,15},{1,0},{2,1},{3,2},{4,3},{5,4},{6,5},{7,6},{8,7},{9,8},{10,9... | collective-permute-start | bytes 884744 | tf_op jit(solution)/shard_map/ppermute | solution.py:18
  347.6 3.6 collective-permute-done.8
  351.3 5.6 %collective-permute-start.11 = (bf16[1,48,3072]{2,1,0:T(8,128)(2,1)S(1)}, bf16[1,48,3072]{2,1,0:T(8,128)(2,1)S(1)}, u32[]{:S(2)}, u32[]{:S(2)}) collective-permute-start(bf16[1,48,3072]{2,1,0:T(8,128)(2,1)S(1)} %collective-permute-done.9), channel_id=1, source_target_pairs={{0,15},{1,0},{2,1},{3,2},{4,3},{5,4},{6,5},{7,6},{8,7},{9,8},{10,9... | collective-permute-start | bytes 884744 | tf_op jit(solution)/shard_map/ppermute | solution.py:18
  358.4 4.4 %collective-permute-done.10 = bf16[1,48,3072]{2,1,0:T(8,128)(2,1)S(1)} collective-permute-done((bf16[1,48,3072]{2,1,0:T(8,128)(2,1)S(1)}, bf16[1,48,3072]{2,1,0:T(8,128)(2,1)S(1)}, u32[]{:S(2)}, u32[]{:S(2)}) %collective-permute-start.10) | collective-permute-done | bytes 294944 | tf_op jit(solution)/shard_map/ppermute | solution.py:15
  362.9 5.8 %collective-permute-start.13 = (bf16[1,48,3072]{2,1,0:T(8,128)(2,1)S(1)}, bf16[1,48,3072]{2,1,0:T(8,128)(2,1)S(1)}, u32[]{:S(2)}, u32[]{:S(2)}) collective-permute-start(bf16[1,48,3072]{2,1,0:T(8,128)(2,1)S(1)} %collective-permute-done.11), channel_id=1, source_target_pairs={{0,15},{1,0},{2,1},{3,2},{4,3},{5,4},{6,5},{7,6},{8,7},{9,8},{10,9... | collective-permute-start | bytes 884744 | tf_op jit(solution)/shard_map/ppermute | solution.py:18
  370.2 5.3 %collective-permute-done.12 = bf16[1,48,3072]{2,1,0:T(8,128)(2,1)S(1)} collective-permute-done((bf16[1,48,3072]{2,1,0:T(8,128)(2,1)S(1)}, bf16[1,48,3072]{2,1,0:T(8,128)(2,1)S(1)}, u32[]{:S(2)}, u32[]{:S(2)}) %collective-permute-start.12) | collective-permute-done | bytes 294944 | tf_op jit(solution)/shard_map/ppermute | solution.py:15
  377.0 8.5 %collective-permute-done.14 = bf16[1,48,3072]{2,1,0:T(8,128)(2,1)S(1)} collective-permute-done((bf16[1,48,3072]{2,1,0:T(8,128)(2,1)S(1)}, bf16[1,48,3072]{2,1,0:T(8,128)(2,1)S(1)}, u32[]{:S(2)}, u32[]{:S(2)}) %collective-permute-start.14) | collective-permute-done | bytes 294944 | tf_op jit(solution)/shard_map/ppermute | solution.py:15
  386.3 4.4 %gather_fusion = bf16[8,48,3072]{2,1,0:T(8,128)(2,1)} fusion(bf16[16,48,3072]{2,1,0:T(8,128)(2,1)} %constant_dynamic-update-slice_fusion, s32[1024]{0:T(1024)S(1)} %pad_clamp_fusion), kind=kCustom, calls=%fused_computation | custom fusion | bytes 4718624 | tf_op jit(solution)/shard_map/jit(_take)/gather | solution.py:87
  390.7 3.4 broadcast_select_fusion
  (68 shorter events, 15.8 us)
Async XLA Ops:
  7.2 1.4 copy-start
  7.2 52.8 %copy-start.6 = (f32[8,32,32]{2,1,0:T(8,128)S(1)}, f32[8,32,32]{2,1,0:T(8,128)}, u32[]{:S(2)}) copy-start(f32[8,32,32]{2,1,0:T(8,128)} %param.13) | copy-start | bytes 98308
  7.2 178.5 %all-reduce.5.cloned.1.call-start = ((), (), s32[]{:S(2)}) async-start(), calls=%async_computation.1 | async-start | bytes 6291456
  69.4 9.5 %copy-start.11 = (u32[256]{0:T(256)S(1)}, u32[256]{0:T(256)}, u32[]{:S(2)}) copy-start(u32[256]{0:T(256)} %constant.203) | copy-start | bytes 3076
  69.4 10.8 %copy-start.9 = (f32[1,672]{1,0:T(1,128)S(1)}, f32[1,672]{1,0:T(1,128)}, u32[]{:S(2)}) copy-start(f32[1,672]{1,0:T(1,128)} %param.17) | copy-start | bytes 8068
  69.4 165.4 %copy-start.10 = (s32[8]{0:T(128)S(1)}, s32[8]{0:T(128)}, u32[]{:S(2)}) copy-start(s32[8]{0:T(128)} %param.14) | copy-start | bytes 100
  78.8 185.8 %copy-start.7 = (f32[672]{0:T(1024)S(1)}, f32[672]{0:T(1024)}, u32[]{:S(2)}) copy-start(f32[672]{0:T(1024)} %param.19) | copy-start | bytes 8068
  78.8 185.8 %copy-start.8 = (f32[672]{0:T(1024)S(1)}, f32[672]{0:T(1024)}, u32[]{:S(2)}) copy-start(f32[672]{0:T(1024)} %param.18) | copy-start | bytes 8068
  78.9 205.0 %all-gather.2.cloned.1.call-start = ((), (), s32[]{:S(2)}) async-start(), calls=%async_computation | async-start | bytes 1671168 | tf_op jit(solution)/shard_map/all_gather | solution.py:66
  238.8 52.8 %copy-start.5 = (f32[1,1,48,3072]{3,2,1,0:T(8,128)S(1)}, f32[1,1,48,3072]{3,2,1,0:T(8,128)}, u32[]{:S(2)}) copy-start(f32[1,1,48,3072]{3,2,1,0:T(8,128)} %param.15) | copy-start | bytes 1769476
  265.3 29.5 %copy-start.4 = (f32[1,1,48,3072]{3,2,1,0:T(8,128)S(1)}, f32[1,1,48,3072]{3,2,1,0:T(8,128)}, u32[]{:S(2)}) copy-start(f32[1,1,48,3072]{3,2,1,0:T(8,128)} %param.16) | copy-start | bytes 1769476
  291.6 13.1 %copy-start.1 = (bf16[8,3072,32]{2,1,0:T(8,128)(2,1)S(1)}, bf16[8,3072,32]{2,1,0:T(8,128)(2,1)}, u32[]{:S(2)}) copy-start(bf16[8,3072,32]{2,1,0:T(8,128)(2,1)} %reshape.77) | copy-start | bytes 4718596
  291.6 13.1 %copy-start.2 = (bf16[1,8,48,3072]{3,2,1,0:T(8,128)(2,1)S(1)}, bf16[1,8,48,3072]{3,2,1,0:T(8,128)(2,1)}, u32[]{:S(2)}) copy-start(bf16[1,8,48,3072]{3,2,1,0:T(8,128)(2,1)} %param.11) | copy-start | bytes 7077892
  294.7 15.4 %copy-start.3 = (f32[48,3072]{1,0:T(8,128)}, f32[48,3072]{1,0:T(8,128)S(1)}, u32[]{:S(2)}) copy-start(f32[48,3072]{1,0:T(8,128)S(1)} %convolution_add_fusion) | copy-start | bytes 1769476
  299.4 11.1 %collective-permute-start = (bf16[1,48,3072]{2,1,0:T(8,128)(2,1)S(1)}, bf16[1,48,3072]{2,1,0:T(8,128)(2,1)S(1)}, u32[]{:S(2)}, u32[]{:S(2)}) collective-permute-start(bf16[1,48,3072]{2,1,0:T(8,128)(2,1)S(1)} %get-tuple-element.37), channel_id=1, source_target_pairs={{0,1},{1,2},{2,3},{3,4},{4,5},{5,6},{6,7},{7,8},{8,9},{9,10},{10,1... | collective-permute-start | bytes 884744 | tf_op jit(solution)/shard_map/ppermute | solution.py:15
  300.5 10.0 %collective-permute-start.1 = (bf16[1,48,3072]{2,1,0:T(8,128)(2,1)S(1)}, bf16[1,48,3072]{2,1,0:T(8,128)(2,1)S(1)}, u32[]{:S(2)}, u32[]{:S(2)}) collective-permute-start(bf16[1,48,3072]{2,1,0:T(8,128)(2,1)S(1)} %get-tuple-element.37), channel_id=1, source_target_pairs={{0,15},{1,0},{2,1},{3,2},{4,3},{5,4},{6,5},{7,6},{8,7},{9,8},{10,9... | collective-permute-start | bytes 884744 | tf_op jit(solution)/shard_map/ppermute | solution.py:18
  310.5 10.2 %collective-permute-start.2 = (bf16[1,48,3072]{2,1,0:T(8,128)(2,1)S(1)}, bf16[1,48,3072]{2,1,0:T(8,128)(2,1)S(1)}, u32[]{:S(2)}, u32[]{:S(2)}) collective-permute-start(bf16[1,48,3072]{2,1,0:T(8,128)(2,1)S(1)} %collective-permute-done), channel_id=1, source_target_pairs={{0,1},{1,2},{2,3},{3,4},{4,5},{5,6},{6,7},{7,8},{8,9},{9,10},{10,1... | collective-permute-start | bytes 884744 | tf_op jit(solution)/shard_map/ppermute | solution.py:15
  310.5 10.2 %collective-permute-start.3 = (bf16[1,48,3072]{2,1,0:T(8,128)(2,1)S(1)}, bf16[1,48,3072]{2,1,0:T(8,128)(2,1)S(1)}, u32[]{:S(2)}, u32[]{:S(2)}) collective-permute-start(bf16[1,48,3072]{2,1,0:T(8,128)(2,1)S(1)} %collective-permute-done.1), channel_id=1, source_target_pairs={{0,15},{1,0},{2,1},{3,2},{4,3},{5,4},{6,5},{7,6},{8,7},{9,8},{10,9... | collective-permute-start | bytes 884744 | tf_op jit(solution)/shard_map/ppermute | solution.py:18
  320.7 10.0 %collective-permute-start.4 = (bf16[1,48,3072]{2,1,0:T(8,128)(2,1)S(1)}, bf16[1,48,3072]{2,1,0:T(8,128)(2,1)S(1)}, u32[]{:S(2)}, u32[]{:S(2)}) collective-permute-start(bf16[1,48,3072]{2,1,0:T(8,128)(2,1)S(1)} %collective-permute-done.2), channel_id=1, source_target_pairs={{0,1},{1,2},{2,3},{3,4},{4,5},{5,6},{6,7},{7,8},{8,9},{9,10},{10,1... | collective-permute-start | bytes 884744 | tf_op jit(solution)/shard_map/ppermute | solution.py:15
  320.7 10.0 %collective-permute-start.5 = (bf16[1,48,3072]{2,1,0:T(8,128)(2,1)S(1)}, bf16[1,48,3072]{2,1,0:T(8,128)(2,1)S(1)}, u32[]{:S(2)}, u32[]{:S(2)}) collective-permute-start(bf16[1,48,3072]{2,1,0:T(8,128)(2,1)S(1)} %collective-permute-done.3), channel_id=1, source_target_pairs={{0,15},{1,0},{2,1},{3,2},{4,3},{5,4},{6,5},{7,6},{8,7},{9,8},{10,9... | collective-permute-start | bytes 884744 | tf_op jit(solution)/shard_map/ppermute | solution.py:18
  330.8 10.0 %collective-permute-start.6 = (bf16[1,48,3072]{2,1,0:T(8,128)(2,1)S(1)}, bf16[1,48,3072]{2,1,0:T(8,128)(2,1)S(1)}, u32[]{:S(2)}, u32[]{:S(2)}) collective-permute-start(bf16[1,48,3072]{2,1,0:T(8,128)(2,1)S(1)} %collective-permute-done.4), channel_id=1, source_target_pairs={{0,1},{1,2},{2,3},{3,4},{4,5},{5,6},{6,7},{7,8},{8,9},{9,10},{10,1... | collective-permute-start | bytes 884744 | tf_op jit(solution)/shard_map/ppermute | solution.py:15
  330.8 10.0 %collective-permute-start.7 = (bf16[1,48,3072]{2,1,0:T(8,128)(2,1)S(1)}, bf16[1,48,3072]{2,1,0:T(8,128)(2,1)S(1)}, u32[]{:S(2)}, u32[]{:S(2)}) collective-permute-start(bf16[1,48,3072]{2,1,0:T(8,128)(2,1)S(1)} %collective-permute-done.5), channel_id=1, source_target_pairs={{0,15},{1,0},{2,1},{3,2},{4,3},{5,4},{6,5},{7,6},{8,7},{9,8},{10,9... | collective-permute-start | bytes 884744 | tf_op jit(solution)/shard_map/ppermute | solution.py:18
  340.8 10.4 %collective-permute-start.8 = (bf16[1,48,3072]{2,1,0:T(8,128)(2,1)S(1)}, bf16[1,48,3072]{2,1,0:T(8,128)(2,1)S(1)}, u32[]{:S(2)}, u32[]{:S(2)}) collective-permute-start(bf16[1,48,3072]{2,1,0:T(8,128)(2,1)S(1)} %collective-permute-done.6), channel_id=1, source_target_pairs={{0,1},{1,2},{2,3},{3,4},{4,5},{5,6},{6,7},{7,8},{8,9},{9,10},{10,1... | collective-permute-start | bytes 884744 | tf_op jit(solution)/shard_map/ppermute | solution.py:15
  340.8 10.4 %collective-permute-start.9 = (bf16[1,48,3072]{2,1,0:T(8,128)(2,1)S(1)}, bf16[1,48,3072]{2,1,0:T(8,128)(2,1)S(1)}, u32[]{:S(2)}, u32[]{:S(2)}) collective-permute-start(bf16[1,48,3072]{2,1,0:T(8,128)(2,1)S(1)} %collective-permute-done.7), channel_id=1, source_target_pairs={{0,15},{1,0},{2,1},{3,2},{4,3},{5,4},{6,5},{7,6},{8,7},{9,8},{10,9... | collective-permute-start | bytes 884744 | tf_op jit(solution)/shard_map/ppermute | solution.py:18
  351.2 11.5 %collective-permute-start.10 = (bf16[1,48,3072]{2,1,0:T(8,128)(2,1)S(1)}, bf16[1,48,3072]{2,1,0:T(8,128)(2,1)S(1)}, u32[]{:S(2)}, u32[]{:S(2)}) collective-permute-start(bf16[1,48,3072]{2,1,0:T(8,128)(2,1)S(1)} %collective-permute-done.8), channel_id=1, source_target_pairs={{0,1},{1,2},{2,3},{3,4},{4,5},{5,6},{6,7},{7,8},{8,9},{9,10},{10,1... | collective-permute-start | bytes 884744 | tf_op jit(solution)/shard_map/ppermute | solution.py:15
  351.3 11.6 %collective-permute-start.11 = (bf16[1,48,3072]{2,1,0:T(8,128)(2,1)S(1)}, bf16[1,48,3072]{2,1,0:T(8,128)(2,1)S(1)}, u32[]{:S(2)}, u32[]{:S(2)}) collective-permute-start(bf16[1,48,3072]{2,1,0:T(8,128)(2,1)S(1)} %collective-permute-done.9), channel_id=1, source_target_pairs={{0,15},{1,0},{2,1},{3,2},{4,3},{5,4},{6,5},{7,6},{8,7},{9,8},{10,9... | collective-permute-start | bytes 884744 | tf_op jit(solution)/shard_map/ppermute | solution.py:18
  362.8 12.7 %collective-permute-start.12 = (bf16[1,48,3072]{2,1,0:T(8,128)(2,1)S(1)}, bf16[1,48,3072]{2,1,0:T(8,128)(2,1)S(1)}, u32[]{:S(2)}, u32[]{:S(2)}) collective-permute-start(bf16[1,48,3072]{2,1,0:T(8,128)(2,1)S(1)} %collective-permute-done.10), channel_id=1, source_target_pairs={{0,1},{1,2},{2,3},{3,4},{4,5},{5,6},{6,7},{7,8},{8,9},{9,10},{10,1... | collective-permute-start | bytes 884744 | tf_op jit(solution)/shard_map/ppermute | solution.py:15
  362.9 13.4 %collective-permute-start.13 = (bf16[1,48,3072]{2,1,0:T(8,128)(2,1)S(1)}, bf16[1,48,3072]{2,1,0:T(8,128)(2,1)S(1)}, u32[]{:S(2)}, u32[]{:S(2)}) collective-permute-start(bf16[1,48,3072]{2,1,0:T(8,128)(2,1)S(1)} %collective-permute-done.11), channel_id=1, source_target_pairs={{0,15},{1,0},{2,1},{3,2},{4,3},{5,4},{6,5},{7,6},{8,7},{9,8},{10,9... | collective-permute-start | bytes 884744 | tf_op jit(solution)/shard_map/ppermute | solution.py:18
  375.5 10.0 %collective-permute-start.14 = (bf16[1,48,3072]{2,1,0:T(8,128)(2,1)S(1)}, bf16[1,48,3072]{2,1,0:T(8,128)(2,1)S(1)}, u32[]{:S(2)}, u32[]{:S(2)}) collective-permute-start(bf16[1,48,3072]{2,1,0:T(8,128)(2,1)S(1)} %collective-permute-done.12), channel_id=1, source_target_pairs={{0,1},{1,2},{2,3},{3,4},{4,5},{5,6},{6,7},{7,8},{8,9},{9,10},{10,1... | collective-permute-start | bytes 884744 | tf_op jit(solution)/shard_map/ppermute | solution.py:15
Sparse Core Ops, SparseCore 0:
  79.0 106.7 all-reduce.4
  234.5 49.2 all-gather.1
